TPU v7x, 128 devices: a whole 4x4x4 slice. The times are simulated.
128 devices in a mesh: row: 8 (over z, x_lo), col: 16 (over x_hi, y, core).
Axes of the slice: x: 4 (x_hi: 2, x_lo: 2; x = x_hi * 2 + x_lo), y: 4, z: 4, core: 2. Of those that a mesh axis runs over, the one named last changes fastest.
Arguments:
- blocks: bfloat16 [8, 16, 192, 128, 128], P('row', 'col'), may hold values from -0.059814453 to 0.059814453
- block_rows: int32 [8, 16, 192], P('row', 'col'), may hold values from 0 to 255, as said below
- block_cols: int32 [8, 16, 192], P('row', 'col'), may hold values from 0 to 255, as said below
- counts: int32 [8, 16], P('row', 'col'), may hold values from 96 to 192, as said below
- travel_times: float32 [16, 262144], P(None, ('row', 'col')), may hold values from -6 to 6
Outputs:
- solution: float32 [16, 16, 8, 4096], P(None, 'col', 'row')
- scaled_direction: float32 [16, 16, 8, 4096], P(None, 'col', 'row')
Inputs may be any that keep to these rules, and one draw needn't show every extreme that they name: Ray block of a slot within the 256 ray blocks of its row group; among the filled slots of one device the (block_rows, block_cols) pairs are all different. `block_cols`: cell block of a slot within the 256 cell blocks of its column group. `counts`: some device fills all 192 slots.
All inputs are finite; a program needn't handle non-finite values.
Results may differ from a plain program's by a relative error of at most 0.0054.
Values may be sent and summed in bfloat16 or wider, within the bound.
No kernel may reach another device: no remote copies, remote signals or barrier semaphores. Data moves between devices by JAX's collectives and lax.ppermute only.
A program may use at most 64 MiB of HBM per device.

v0:
```python
import jax
import jax.numpy as jnp
from jax import lax
from jax.sharding import PartitionSpec as P

RB_DEV = 256
CB_DEV = 256
ITERS = 2
norm_eps = 1e-06


def rotation(rho_bar, phi_bar, beta_norm, alpha_norm):
    rho_new = jnp.sqrt(rho_bar * rho_bar + beta_norm * beta_norm)
    cosine = rho_bar / rho_new
    sine_val = beta_norm / rho_new
    theta_coef = sine_val * alpha_norm
    rho_next = -cosine * alpha_norm
    phi_new = cosine * phi_bar
    phi_next = sine_val * phi_bar
    return (phi_new / rho_new, theta_coef / rho_new, rho_next, phi_next)


def forward_rows(right_full, blocks_here, cols_here, row_hot):
    count_rhs = right_full.shape[0]
    block_size = blocks_here.shape[1]
    cells = right_full.reshape(count_rhs, right_full.shape[1] // block_size, block_size)
    picked = jnp.take(cells, cols_here, axis=1)
    product = jnp.einsum("knj,nij->kni", picked, blocks_here, preferred_element_type=jnp.float32)
    summed = jnp.einsum("rn,kni->kri", row_hot, product, precision=lax.Precision.HIGHEST)
    return summed.reshape(count_rhs, -1)


def backward_cols(left_full, blocks_here, rows_here, col_hot):
    count_rhs = left_full.shape[0]
    block_size = blocks_here.shape[1]
    rays = left_full.reshape(count_rhs, left_full.shape[1] // block_size, block_size)
    picked = jnp.take(rays, rows_here, axis=1)
    product = jnp.einsum("kni,nij->knj", picked, blocks_here, preferred_element_type=jnp.float32)
    summed = jnp.einsum("cn,knj->kcj", col_hot, product, precision=lax.Precision.HIGHEST)
    return summed.reshape(count_rhs, -1)


def square_sums(values):
    return jnp.sum(values * values, axis=1)


def shards(blocks, block_rows, block_cols, counts, travel_times):
    blocks_here = blocks[0, 0]
    rows_here = block_rows[0, 0]
    cols_here = block_cols[0, 0]
    slots = jnp.arange(blocks_here.shape[0], dtype=jnp.int32)
    filled = slots < counts[0, 0]
    row_hot = (
        (rows_here[None, :] == jnp.arange(RB_DEV, dtype=jnp.int32)[:, None]) & filled[None, :]
    ).astype(jnp.float32)
    col_hot = (
        (cols_here[None, :] == jnp.arange(CB_DEV, dtype=jnp.int32)[:, None]) & filled[None, :]
    ).astype(jnp.float32)
    count_rhs = travel_times.shape[0]

    def global_norm(partial_value):
        return jnp.sqrt(lax.psum(square_sums(partial_value), ("row", "col")) + norm_eps)

    def ray_side(partial_value):
        beta_norm = global_norm(partial_value)
        left_full = lax.all_gather(
            (partial_value / beta_norm[:, None]).astype(jnp.bfloat16), "col", axis=1, tiled=True
        )
        return (partial_value / beta_norm[:, None], left_full, beta_norm)

    def cell_side(partial_value):
        alpha_norm = global_norm(partial_value)
        right_full = None
        return (partial_value / alpha_norm[:, None], right_full, alpha_norm)

    def rows_to_cells(left_full):
        partial_value = backward_cols(left_full, blocks_here, rows_here, col_hot)
        return lax.psum_scatter(partial_value, "row", scatter_dimension=1, tiled=True)

    left_vec, left_full, beta_norm = ray_side(travel_times)
    right_vec, right_full, alpha_norm = cell_side(rows_to_cells(left_full))
    direction = right_vec
    solution = jnp.zeros_like(right_vec)
    phi_bar = beta_norm
    rho_bar = alpha_norm
    for iteration in range(ITERS):
        cells_right_full = lax.all_gather(right_vec.astype(jnp.bfloat16), "row", axis=1, tiled=True)
        cells_partial_value = forward_rows(cells_right_full, blocks_here, cols_here, row_hot)
        left_vec, left_full, beta_norm = ray_side(
            lax.psum_scatter(cells_partial_value, "col", scatter_dimension=1, tiled=True)
            - alpha_norm[:, None] * left_vec
        )
        right_vec, right_full, alpha_norm = cell_side(
            rows_to_cells(left_full) - beta_norm[:, None] * right_vec
        )
        step_scale, turn_scale, rho_bar, phi_bar = rotation(rho_bar, phi_bar, beta_norm, alpha_norm)
        solution = solution + step_scale[:, None] * direction
        direction = right_vec - turn_scale[:, None] * direction
    scaled = phi_bar[:, None] * direction
    return (solution.reshape(count_rhs, 1, 1, -1), scaled.reshape(count_rhs, 1, 1, -1))


def solution(mesh):
    placed = (
        P("row", "col", None, None, None),
        P("row", "col", None),
        P("row", "col", None),
        P("row", "col"),
        P(None, ("row", "col")),
    )
    return jax.shard_map(
        shards,
        mesh=mesh,
        in_specs=placed,
        out_specs=(P(None, "col", "row", None), P(None, "col", "row", None)),
        check_vma=False,
    )
```

profile of v0, /device:TPU:1, one launch (start us, length us, event | category | flops | bytes accessed | tf_op | source)
XLA Modules:
  0.0 989.8 jit_solution(17914631215639586107)
XLA Ops:
  7.2 1.0 multiply_reduce_fusion.5
  8.2 68.7 %psum.42 = f32[16]{0:T(128)S(1)} all-reduce(f32[16]{0:T(128)S(1)} %multiply_reduce_fusion.5), channel_id=1, replica_groups=mesh['row'=8,'col'=16] {'row','col'}, use_global_device_ids=true, to_apply=%region_1.0 | all-reduce | flops 16 | bytes 128 | tf_op jit(solution)/shard_map/psum | solution.py:62
  76.9 1.6 fusion.69
  79.3 0.7 compare_select_fusion.1
  80.0 0.7 compare_and_fusion.1
  80.7 39.5 %all-gather.6.cloned.1.call-done = bf16[16,32768]{1,0:T(8,128)(2,1)} async-done(((bf16[16,2048]{1,0:T(8,128)(2,1)}), bf16[16,32768]{1,0:T(8,128)(2,1)}) %all-gather.6.cloned.1.call-update) | async-done | bytes 1048592 | tf_op jit(solution)/shard_map/all_gather | solution.py:66
  120.1 1.4 copy_bitcast_fusion.9
  121.5 0.8 gather_fusion
  122.3 3.9 fusion.15
  126.3 2.0 convolution_bitcast_fusion.4
  128.2 1.8 copy.16
  130.1 4.2 copy.65
  134.3 51.0 %reduce-scatter.6.cloned.1.call-done = f32[16,4096]{1,0:T(8,128)} async-done(((f32[16,32768]{1,0:T(8,128)}), f32[16,4096]{1,0:T(8,128)}) %reduce-scatter.6.cloned.1.call-update) | async-done | bytes 262160 | tf_op jit(solution)/shard_map/reduce_scatter | solution.py:78
  185.3 1.1 multiply_reduce_fusion.2
  186.4 64.5 %psum.43 = f32[16]{0:T(128)S(1)} all-reduce(f32[16]{0:T(128)S(1)} %multiply_reduce_fusion.2), channel_id=1, replica_groups=mesh['row'=8,'col'=16] {'row','col'}, use_global_device_ids=true, to_apply=%region_4.6 | all-reduce | flops 16 | bytes 128 | tf_op jit(solution)/shard_map/psum | solution.py:62
  250.9 1.7 fusion.79
  252.7 0.2 reduce-scatter.8.cloned.1.call-start
  252.9 32.9 %all-gather.8.cloned.1.call-done = bf16[16,32768]{1,0:T(8,128)(2,1)} async-done(((bf16[16,4096]{1,0:T(8,128)(2,1)}), bf16[16,32768]{1,0:T(8,128)(2,1)}) %all-gather.8.cloned.1.call-update) | async-done | bytes 1048592 | tf_op jit(solution)/shard_map/all_gather | solution.py:87
  285.8 1.4 copy_bitcast_fusion.8
  287.2 0.8 gather_fusion.1
  288.0 5.5 fusion.18
  293.5 2.0 convolution_bitcast_fusion.3
  295.5 1.8 copy.19
  297.3 4.2 copy.64
  301.6 73.0 %reduce-scatter.8.cloned.1.call-done = f32[16,2048]{1,0:T(8,128)} async-done(((f32[16,32768]{1,0:T(8,128)}), f32[16,2048]{1,0:T(8,128)}) %reduce-scatter.8.cloned.1.call-update) | async-done | bytes 131088 | tf_op jit(solution)/shard_map/reduce_scatter | solution.py:90
  374.6 1.1 multiply_reduce_fusion.4
  375.7 66.4 %psum.44 = f32[16]{0:T(128)S(1)} all-reduce(f32[16]{0:T(128)S(1)} %get-tuple-element.17), channel_id=1, replica_groups=mesh['row'=8,'col'=16] {'row','col'}, use_global_device_ids=true, to_apply=%region_7.9 | all-reduce | flops 16 | bytes 128 | tf_op jit(solution)/shard_map/psum | solution.py:62
  442.1 0.7 fusion.70
  442.9 41.6 %all-gather.10.cloned.1.call-done = bf16[16,32768]{1,0:T(8,128)(2,1)} async-done(((bf16[16,2048]{1,0:T(8,128)(2,1)}), bf16[16,32768]{1,0:T(8,128)(2,1)}) %all-gather.10.cloned.1.call-update) | async-done | bytes 1048592 | tf_op jit(solution)/shard_map/all_gather | solution.py:66
  484.5 1.4 copy_bitcast_fusion.7
  485.9 0.8 gather_fusion.2
  486.7 3.9 fusion.21
  490.6 2.0 convolution_bitcast_fusion.2
  492.6 1.8 copy.22
  494.4 4.2 copy.63
  498.6 51.0 %reduce-scatter.10.cloned.1.call-done = f32[16,4096]{1,0:T(8,128)} async-done(((f32[16,32768]{1,0:T(8,128)}), f32[16,4096]{1,0:T(8,128)}) %reduce-scatter.10.cloned.1.call-update) | async-done | bytes 262160 | tf_op jit(solution)/shard_map/reduce_scatter | solution.py:78
  549.6 1.2 multiply_reduce_fusion.1
  550.8 64.8 %psum.45 = f32[16]{0:T(128)S(1)} all-reduce(f32[16]{0:T(128)S(1)} %multiply_reduce_fusion.1), channel_id=1, replica_groups=mesh['row'=8,'col'=16] {'row','col'}, use_global_device_ids=true, to_apply=%region_10.12 | all-reduce | flops 16 | bytes 128 | tf_op jit(solution)/shard_map/psum | solution.py:62
  615.6 1.7 fusion.83
  617.4 33.1 %all-gather.12.cloned.1.call-done = bf16[16,32768]{1,0:T(8,128)(2,1)} async-done(((bf16[16,4096]{1,0:T(8,128)(2,1)}), bf16[16,32768]{1,0:T(8,128)(2,1)}) %all-gather.12.cloned.1.call-update) | async-done | bytes 1048592 | tf_op jit(solution)/shard_map/all_gather | solution.py:87
  650.5 1.4 copy_bitcast_fusion.6
  651.9 0.8 gather_fusion.3
  652.7 5.5 fusion.24
  658.2 2.0 convolution_bitcast_fusion.1
  660.2 1.8 copy.25
  662.0 4.2 copy.62
  666.2 73.0 %reduce-scatter.12.cloned.1.call-done = f32[16,2048]{1,0:T(8,128)} async-done(((f32[16,32768]{1,0:T(8,128)}), f32[16,2048]{1,0:T(8,128)}) %reduce-scatter.12.cloned.1.call-update) | async-done | bytes 131088 | tf_op jit(solution)/shard_map/reduce_scatter | solution.py:90
  739.2 1.1 multiply_reduce_fusion.3
  740.3 66.4 %psum.46 = f32[16]{0:T(128)S(1)} all-reduce(f32[16]{0:T(128)S(1)} %get-tuple-element.13), channel_id=1, replica_groups=mesh['row'=8,'col'=16] {'row','col'}, use_global_device_ids=true, to_apply=%region_13.15 | all-reduce | flops 16 | bytes 128 | tf_op jit(solution)/shard_map/psum | solution.py:62
  806.8 0.7 divide_convert_fusion
  807.5 0.3 reduce-scatter.14.cloned.1.call-start
  807.8 41.2 %all-gather.14.cloned.1.call-done = bf16[16,32768]{1,0:T(8,128)(2,1)} async-done(((bf16[16,2048]{1,0:T(8,128)(2,1)}), bf16[16,32768]{1,0:T(8,128)(2,1)}) %all-gather.14.cloned.1.call-update) | async-done | bytes 1048592 | tf_op jit(solution)/shard_map/all_gather | solution.py:66
  849.0 1.4 copy_bitcast_fusion.5
  850.5 0.8 gather_fusion.4
  851.2 3.9 fusion.27
  855.1 2.0 convolution_bitcast_fusion
  857.1 1.8 copy.28
  859.0 4.2 copy.61
  863.1 51.1 %reduce-scatter.14.cloned.1.call-done = f32[16,4096]{1,0:T(8,128)} async-done(((f32[16,32768]{1,0:T(8,128)}), f32[16,4096]{1,0:T(8,128)}) %reduce-scatter.14.cloned.1.call-update) | async-done | bytes 262160 | tf_op jit(solution)/shard_map/reduce_scatter | solution.py:78
  914.2 1.2 multiply_reduce_fusion
  915.4 64.5 %psum.47 = f32[16]{0:T(128)S(1)} all-reduce(f32[16]{0:T(128)S(1)} %multiply_reduce_fusion), channel_id=1, replica_groups=mesh['row'=8,'col'=16] {'row','col'}, use_global_device_ids=true, to_apply=%region_16.18 | all-reduce | flops 16 | bytes 128 | tf_op jit(solution)/shard_map/psum | solution.py:62
  979.9 1.1 multiply_bitcast_fusion
  981.0 1.0 copy.30
  982.0 1.0 copy.29
  (37 shorter events, 0.6 us)
Async XLA Ops:
  7.2 113.0 %all-gather.6.cloned.1.call-start = ((), (), s32[]{:S(2)}) async-start(), calls=%async_computation.5 | async-start | bytes 1114112 | tf_op jit(solution)/shard_map/all_gather | solution.py:66
  78.6 106.7 %reduce-scatter.6.cloned.1.call-start = ((), (), s32[]{:S(2)}) async-start(), calls=%async_computation.6 | async-start | bytes 2359296 | tf_op jit(solution)/shard_map/reduce_scatter | solution.py:78
  122.3 3.9 copy-start.2
  134.3 151.6 %all-gather.8.cloned.1.call-start = ((), (), s32[]{:S(2)}) async-start(), calls=%async_computation.7 | async-start | bytes 1179648 | tf_op jit(solution)/shard_map/all_gather | solution.py:87
  252.7 121.9 %reduce-scatter.8.cloned.1.call-start = ((), (), s32[]{:S(2)}) async-start(), calls=%async_computation.8 | async-start | bytes 2228224 | tf_op jit(solution)/shard_map/reduce_scatter | solution.py:90
  288.0 5.5 copy-start.3
  301.5 73.1 %copy-start.1 = (f32[16,2048]{1,0:T(8,128)S(1)}, f32[16,2048]{1,0:T(8,128)}, u32[]{:S(2)}) copy-start(f32[16,2048]{1,0:T(8,128)} %param.11) | copy-start | bytes 393220
  301.5 183.0 %all-gather.10.cloned.1.call-start = ((), (), s32[]{:S(2)}) async-start(), calls=%async_computation.9 | async-start | bytes 1114112 | tf_op jit(solution)/shard_map/all_gather | solution.py:66
  442.9 106.8 %reduce-scatter.10.cloned.1.call-start = ((), (), s32[]{:S(2)}) async-start(), calls=%async_computation.10 | async-start | bytes 2359296 | tf_op jit(solution)/shard_map/reduce_scatter | solution.py:78
  498.6 51.1 %copy-start = (f32[16,4096]{1,0:T(8,128)S(1)}, f32[16,4096]{1,0:T(8,128)}, u32[]{:S(2)}) copy-start(f32[16,4096]{1,0:T(8,128)} %reduce-scatter.6.cloned.1.call-done) | copy-start | bytes 786436
  498.6 151.9 %all-gather.12.cloned.1.call-start = ((), (), s32[]{:S(2)}) async-start(), calls=%async_computation.11 | async-start | bytes 1179648 | tf_op jit(solution)/shard_map/all_gather | solution.py:87
  617.3 121.9 %reduce-scatter.12.cloned.1.call-start = ((), (), s32[]{:S(2)}) async-start(), calls=%async_computation.12 | async-start | bytes 2228224 | tf_op jit(solution)/shard_map/reduce_scatter | solution.py:90
  666.2 182.9 %all-gather.14.cloned.1.call-start = ((), (), s32[]{:S(2)}) async-start(), calls=%async_computation.13 | async-start | bytes 1114112 | tf_op jit(solution)/shard_map/all_gather | solution.py:66
  807.5 106.7 %reduce-scatter.14.cloned.1.call-start = ((), (), s32[]{:S(2)}) async-start(), calls=%async_computation.14 | async-start | bytes 2359296 | tf_op jit(solution)/shard_map/reduce_scatter | solution.py:78
Sparse Core Ops, SparseCore 0:
  78.7 41.3 all-gather.5
  134.4 50.8 reduce-scatter.5
  252.8 32.9 all-gather.7
  301.7 72.8 reduce-scatter.7
  443.0 41.4 all-gather.9
  498.7 50.8 reduce-scatter.9
  617.4 32.9 all-gather.11
  666.3 72.8 reduce-scatter.11
  807.6 41.3 all-gather.13
  863.3 50.8 reduce-scatter.13
where the time goes:
time: 991 us; the launch traced here: 990 us
  waiting for transfers between devices  487 us (49%)
  blocking collectives  395 us (40%)
  local copies, waits for them, and re-layouts  42.8 us (4%)
  matrix products  32.6 us (3%)
  other arithmetic  15.8 us (2%)
  between operations  15 us (2%)
    psum x6, blocking collectives, global_norm(): lax.psum(square_sums(partial_value), ('row', 'col')) + norm_eps  395 us
    reduce_scatter x3, waiting for transfers between devices, rows_to_cells(): lax.psum_scatter(partial_value, 'row', scatter_dimension=1, tiled=True)  153 us
    reduce_scatter x2, waiting for transfers between devices, shards(): lax.psum_scatter(cells_partial_value, 'col', scatter_dimension=1, tiled=T...  146 us
    all_gather x3, waiting for transfers between devices, ray_side(): lax.all_gather((partial_value / beta_norm[:, None]).astype(jnp.bfloat16),...  122 us
    all_gather x2, waiting for transfers between devices, shards(): lax.all_gather(right_vec.astype(jnp.bfloat16), 'row', axis=1, tiled=True)  66 us
    unnamed x15, local copies, waits for them, and re-layouts  22.8 us
  transfers between devices with their start and end apart: 10, of which 10 were waited for; matrix products, arithmetic and copies ran while one was open for 0% of the time, Pallas kernels for 0%

commit v1 on v0

--- a/solution.py
+++ b/solution.py
@@ -63,8 +63,15 @@
 
     def ray_side(partial_value):
         beta_norm = global_norm(partial_value)
-        left_full = lax.all_gather(
-            (partial_value / beta_norm[:, None]).astype(jnp.bfloat16), "col", axis=1, tiled=True
+        panel = (partial_value / beta_norm[:, None]).astype(jnp.bfloat16)
+        left_full = jnp.concatenate(
+            jax.lax.all_to_all(
+                jnp.stack([panel] * jax.lax.axis_size("col")),
+                split_axis=0,
+                axis_name="col",
+                concat_axis=0,
+            ),
+            1,
         )
         return (partial_value / beta_norm[:, None], left_full, beta_norm)
 

time: 991 us -> 931 us (0.939)
  waiting for transfers between devices: 487 us -> 374 us
  blocking collectives: 395 us -> 438 us
    all_gather x3 -> x0, waiting for transfers between devices: 122 us -> none  [ray_side(): lax.all_gather((partial_value / beta_norm[:, None]).astype(jnp.bfloat16),...]
    all_to_all x0 -> x2, blocking collectives: none -> 42.4 us  [ray_side(): jax.lax.all_to_all(jnp.stack([panel] * jax.lax.axis_size('col')), split_a...]
    all_to_all x0 -> x1, waiting for transfers between devices: none -> 16.3 us  [ray_side(): jax.lax.all_to_all(jnp.stack([panel] * jax.lax.axis_size('col')), split_a...]
  transfers between devices with their start and end apart: 10 -> 8, of which waited for: 10 -> 8; matrix products, arithmetic and copies ran while one was open for 0% -> 0% of each run, Pallas kernels for 0% -> 0%
where the time goes in v1:
time: 931 us; the launch traced here: 923 us
  blocking collectives  438 us (47%)
  waiting for transfers between devices  374 us (40%)
  local copies, waits for them, and re-layouts  45.2 us (5%)
  matrix products  32.6 us (4%)
  between operations  15.3 us (2%)
  other arithmetic  12.5 us (1%)
    psum x6, blocking collectives, global_norm(): lax.psum(square_sums(partial_value), ('row', 'col')) + norm_eps  395 us
    reduce_scatter x2, waiting for transfers between devices, shards(): lax.psum_scatter(cells_partial_value, 'col', scatter_dimension=1, tiled=T...  146 us
    reduce_scatter x3, waiting for transfers between devices, rows_to_cells(): lax.psum_scatter(partial_value, 'row', scatter_dimension=1, tiled=True)  146 us
    all_gather x2, waiting for transfers between devices, shards(): lax.all_gather(right_vec.astype(jnp.bfloat16), 'row', axis=1, tiled=True)  65.7 us
    all_to_all x2, blocking collectives, ray_side(): jax.lax.all_to_all(jnp.stack([panel] * jax.lax.axis_size('col')), split_a...  42.4 us
    unnamed x15, local copies, waits for them, and re-layouts  22.8 us
  transfers between devices with their start and end apart: 8, of which 8 were waited for; matrix products, arithmetic and copies ran while one was open for 0% of the time, Pallas kernels for 0%

profile of v1, /device:TPU:1, one launch (start us, length us, event | category | flops | bytes accessed | tf_op | source)
XLA Modules:
  0.0 922.5 jit_solution(2914508300123432339)
XLA Ops:
  7.2 1.0 multiply_reduce_fusion.5
  8.2 68.7 %psum.42 = f32[16]{0:T(128)S(1)} all-reduce(f32[16]{0:T(128)S(1)} %multiply_reduce_fusion.5), channel_id=1, replica_groups=mesh['row'=8,'col'=16] {'row','col'}, use_global_device_ids=true, to_apply=%region_1.0 | all-reduce | flops 16 | bytes 128 | tf_op jit(solution)/shard_map/psum | solution.py:62
  76.9 1.0 fusion.69
  77.9 1.1 stack.6
  79.0 4.8 all-to-all-start
  84.6 16.3 %all-to-all-done = bf16[16,16,2048]{2,1,0:T(8,128)(2,1)S(1)} async-done(((bf16[16,16,2048]{2,1,0:T(8,128)(2,1)}), bf16[16,16,2048]{2,1,0:T(8,128)(2,1)S(1)}, u32[]{:S(2)}, u32[]{:S(2)}) %all-to-all-start) | async-done | bytes 1048608 | tf_op jit(solution)/shard_map/all_to_all | solution.py:68
  100.9 0.6 copy.34
  102.0 0.7 copy.35
  102.7 0.8 gather_fusion
  103.5 3.9 fusion.15
  107.4 2.0 convolution_bitcast_fusion.4
  109.4 1.8 copy.37
  111.2 4.2 copy.82
  115.5 48.2 %reduce-scatter.6.cloned.1.call-done = f32[16,4096]{1,0:T(8,128)} async-done(((f32[16,32768]{1,0:T(8,128)}), f32[16,4096]{1,0:T(8,128)}) %reduce-scatter.6.cloned.1.call-update) | async-done | bytes 262160 | tf_op jit(solution)/shard_map/reduce_scatter | solution.py:85
  163.7 1.1 multiply_reduce_fusion.2
  164.8 64.6 %psum.43 = f32[16]{0:T(128)S(1)} all-reduce(f32[16]{0:T(128)S(1)} %multiply_reduce_fusion.2), channel_id=1, replica_groups=mesh['row'=8,'col'=16] {'row','col'}, use_global_device_ids=true, to_apply=%region_4.6 | all-reduce | flops 16 | bytes 128 | tf_op jit(solution)/shard_map/psum | solution.py:62
  229.4 1.7 fusion.79
  231.5 32.8 %all-gather.3.cloned.1.call-done = bf16[16,32768]{1,0:T(8,128)(2,1)} async-done(((bf16[16,4096]{1,0:T(8,128)(2,1)}), bf16[16,32768]{1,0:T(8,128)(2,1)}) %all-gather.3.cloned.1.call-update) | async-done | bytes 1048592 | tf_op jit(solution)/shard_map/all_gather | solution.py:94
  264.2 1.4 copy_bitcast_fusion.6
  265.6 0.8 gather_fusion.1
  266.4 5.5 fusion.18
  271.9 2.0 convolution_bitcast_fusion.3
  273.9 1.8 copy.40
  275.7 4.2 copy.81
  280.0 73.0 %reduce-scatter.8.cloned.1.call-done = f32[16,2048]{1,0:T(8,128)} async-done(((f32[16,32768]{1,0:T(8,128)}), f32[16,2048]{1,0:T(8,128)}) %reduce-scatter.8.cloned.1.call-update) | async-done | bytes 131088 | tf_op jit(solution)/shard_map/reduce_scatter | solution.py:97
  353.0 1.1 multiply_reduce_fusion.4
  354.1 66.4 %psum.44 = f32[16]{0:T(128)S(1)} all-reduce(f32[16]{0:T(128)S(1)} %get-tuple-element.19), channel_id=1, replica_groups=mesh['row'=8,'col'=16] {'row','col'}, use_global_device_ids=true, to_apply=%region_7.9 | all-reduce | flops 16 | bytes 128 | tf_op jit(solution)/shard_map/psum | solution.py:62
  420.7 21.3 %all_to_all.15 = bf16[16,16,2048]{2,1,0:T(8,128)(2,1)S(1)} all-to-all(bf16[16,16,2048]{2,1,0:T(8,128)(2,1)S(1)} %stack.7), channel_id=1, replica_groups=mesh['row'=8,'col'=16] {'col'}, dimensions={0} | all-to-all | bytes 2097152 | tf_op jit(solution)/shard_map/all_to_all | solution.py:68
  442.0 0.6 copy.41
  442.6 0.5 reshape_reshape.10
  443.2 0.7 copy.42
  443.8 0.8 gather_fusion.2
  444.6 3.9 fusion.21
  448.5 2.0 convolution_bitcast_fusion.2
  450.5 1.8 copy.44
  452.4 4.2 copy.80
  456.6 48.6 %reduce-scatter.10.cloned.1.call-done = f32[16,4096]{1,0:T(8,128)} async-done(((f32[16,32768]{1,0:T(8,128)}), f32[16,4096]{1,0:T(8,128)}) %reduce-scatter.10.cloned.1.call-update) | async-done | bytes 262160 | tf_op jit(solution)/shard_map/reduce_scatter | solution.py:85
  505.2 1.2 multiply_reduce_fusion.1
  506.4 64.6 %psum.45 = f32[16]{0:T(128)S(1)} all-reduce(f32[16]{0:T(128)S(1)} %multiply_reduce_fusion.1), channel_id=1, replica_groups=mesh['row'=8,'col'=16] {'row','col'}, use_global_device_ids=true, to_apply=%region_10.12 | all-reduce | flops 16 | bytes 128 | tf_op jit(solution)/shard_map/psum | solution.py:62
  571.0 1.7 fusion.83
  573.0 32.9 %all-gather.5.cloned.1.call-done = bf16[16,32768]{1,0:T(8,128)(2,1)} async-done(((bf16[16,4096]{1,0:T(8,128)(2,1)}), bf16[16,32768]{1,0:T(8,128)(2,1)}) %all-gather.5.cloned.1.call-update) | async-done | bytes 1048592 | tf_op jit(solution)/shard_map/all_gather | solution.py:94
  605.9 1.4 copy_bitcast_fusion.5
  607.3 0.8 gather_fusion.3
  608.1 5.5 fusion.24
  613.6 2.0 convolution_bitcast_fusion.1
  615.6 1.8 copy.47
  617.4 4.2 copy.79
  621.6 73.0 %reduce-scatter.12.cloned.1.call-done = f32[16,2048]{1,0:T(8,128)} async-done(((f32[16,32768]{1,0:T(8,128)}), f32[16,2048]{1,0:T(8,128)}) %reduce-scatter.12.cloned.1.call-update) | async-done | bytes 131088 | tf_op jit(solution)/shard_map/reduce_scatter | solution.py:97
  694.6 1.1 multiply_reduce_fusion.3
  695.7 66.4 %psum.46 = f32[16]{0:T(128)S(1)} all-reduce(f32[16]{0:T(128)S(1)} %get-tuple-element.15), channel_id=1, replica_groups=mesh['row'=8,'col'=16] {'row','col'}, use_global_device_ids=true, to_apply=%region_13.15 | all-reduce | flops 16 | bytes 128 | tf_op jit(solution)/shard_map/psum | solution.py:62
  762.4 21.0 %all_to_all.16 = bf16[16,16,2048]{2,1,0:T(8,128)(2,1)S(1)} all-to-all(bf16[16,16,2048]{2,1,0:T(8,128)(2,1)S(1)} %stack.8), channel_id=1, replica_groups=mesh['row'=8,'col'=16] {'col'}, dimensions={0} | all-to-all | bytes 2097152 | tf_op jit(solution)/shard_map/all_to_all | solution.py:68
  783.5 0.6 copy.48
  784.6 0.7 copy.49
  785.3 0.8 gather_fusion.4
  786.0 3.9 fusion.27
  789.9 2.0 convolution_bitcast_fusion
  791.9 1.8 copy.51
  793.8 4.2 copy.78
  797.9 48.7 %reduce-scatter.14.cloned.1.call-done = f32[16,4096]{1,0:T(8,128)} async-done(((f32[16,32768]{1,0:T(8,128)}), f32[16,4096]{1,0:T(8,128)}) %reduce-scatter.14.cloned.1.call-update) | async-done | bytes 262160 | tf_op jit(solution)/shard_map/reduce_scatter | solution.py:85
  846.7 1.2 multiply_reduce_fusion
  847.8 64.5 %psum.47 = f32[16]{0:T(128)S(1)} all-reduce(f32[16]{0:T(128)S(1)} %multiply_reduce_fusion), channel_id=1, replica_groups=mesh['row'=8,'col'=16] {'row','col'}, use_global_device_ids=true, to_apply=%region_16.18 | all-reduce | flops 16 | bytes 128 | tf_op jit(solution)/shard_map/psum | solution.py:62
  912.4 1.1 multiply_bitcast_fusion
  913.5 1.0 copy.53
  914.5 1.0 copy.52
  (41 shorter events, 2.4 us)
Async XLA Ops:
  7.2 77.4 %copy-start.3 = (s32[1,1,192]{2,1,0:T(1,128)S(1)}, s32[1,1,192]{2,1,0:T(1,128)}, u32[]{:S(2)}) copy-start(s32[1,1,192]{2,1,0:T(1,128)} %param.8) | copy-start | bytes 2308
  79.0 21.9 %all-to-all-start = ((bf16[16,16,2048]{2,1,0:T(8,128)(2,1)}), bf16[16,16,2048]{2,1,0:T(8,128)(2,1)S(1)}, u32[]{:S(2)}, u32[]{:S(2)}) async-start(bf16[16,16,2048]{2,1,0:T(8,128)(2,1)} %stack.6), calls=%async_computation | async-start | bytes 2097152 | tf_op jit(solution)/shard_map/all_to_all | solution.py:68
  83.8 79.9 %reduce-scatter.6.cloned.1.call-start = ((), (), s32[]{:S(2)}) async-start(), calls=%async_computation.8 | async-start | bytes 2359296 | tf_op jit(solution)/shard_map/reduce_scatter | solution.py:85
  103.5 3.9 copy-start.2
  115.4 148.8 %all-gather.3.cloned.1.call-start = ((), (), s32[]{:S(2)}) async-start(), calls=%async_computation.9 | async-start | bytes 1179648 | tf_op jit(solution)/shard_map/all_gather | solution.py:94
  231.1 121.9 %reduce-scatter.8.cloned.1.call-start = ((), (), s32[]{:S(2)}) async-start(), calls=%async_computation.10 | async-start | bytes 2228224 | tf_op jit(solution)/shard_map/reduce_scatter | solution.py:97
  279.9 73.1 %copy-start.1 = (f32[16,2048]{1,0:T(8,128)S(1)}, f32[16,2048]{1,0:T(8,128)}, u32[]{:S(2)}) copy-start(f32[16,2048]{1,0:T(8,128)} %param.11) | copy-start | bytes 393220
  279.9 225.3 %reduce-scatter.10.cloned.1.call-start = ((), (), s32[]{:S(2)}) async-start(), calls=%async_computation.11 | async-start | bytes 2359296 | tf_op jit(solution)/shard_map/reduce_scatter | solution.py:85
  456.5 48.7 %copy-start = (f32[16,4096]{1,0:T(8,128)S(1)}, f32[16,4096]{1,0:T(8,128)}, u32[]{:S(2)}) copy-start(f32[16,4096]{1,0:T(8,128)} %reduce-scatter.6.cloned.1.call-done) | copy-start | bytes 786436
  456.5 149.4 %all-gather.5.cloned.1.call-start = ((), (), s32[]{:S(2)}) async-start(), calls=%async_computation.12 | async-start | bytes 1179648 | tf_op jit(solution)/shard_map/all_gather | solution.py:94
  572.7 121.9 %reduce-scatter.12.cloned.1.call-start = ((), (), s32[]{:S(2)}) async-start(), calls=%async_computation.13 | async-start | bytes 2228224 | tf_op jit(solution)/shard_map/reduce_scatter | solution.py:97
  621.6 225.1 %reduce-scatter.14.cloned.1.call-start = ((), (), s32[]{:S(2)}) async-start(), calls=%async_computation.14 | async-start | bytes 2359296 | tf_op jit(solution)/shard_map/reduce_scatter | solution.py:85
Sparse Core Ops, SparseCore 0:
  115.5 48.1 reduce-scatter.5
  231.2 32.9 all-gather.2
  280.0 72.8 reduce-scatter.7
  456.7 48.5 reduce-scatter.9
  572.9 32.9 all-gather.4
  621.7 72.8 reduce-scatter.11
  798.1 48.5 reduce-scatter.13
